TPU v7x, 32 devices: a whole 2x2x4 slice. The times are simulated.
32 devices in a mesh: tm: 4 (over y, core), expert: 8 (over z, x).
Axes of the slice: x: 2, y: 2, z: 4, core: 2. Of those that a mesh axis runs over, the one named last changes fastest.
Arguments:
- queries: bfloat16 [4096, 2048], P(('tm', 'expert')), may hold values from -6 to 6
- keys: bfloat16 [4096, 2048], P(('tm', 'expert')), may hold values from -6 to 6
- values: bfloat16 [4096, 2048], P(('tm', 'expert')), may hold values from -6 to 6
- out_grad: bfloat16 [4096, 2048], P(('tm', 'expert')), may hold values from -6 to 6
- expert_ids: int32 [4096, 2], P(('tm', 'expert')), may hold values from 0 to 7, all different within a row
- combine_gates: float32 [4096, 2], P(('tm', 'expert')), may hold values from 0.2 to 1
- gate_weight: bfloat16 [32, 2048, 512], P(('tm', 'expert')), may hold values from -0.125 to 0.125
- up_weight: bfloat16 [32, 2048, 512], P(('tm', 'expert')), may hold values from -0.125 to 0.125
- down_weight: bfloat16 [32, 512, 2048], P(('tm', 'expert')), may hold values from -0.125 to 0.125
Outputs:
- query_grad: bfloat16 [4096, 2048], P(('tm', 'expert'))
- key_grad: bfloat16 [4096, 2048], P(('tm', 'expert'))
- value_grad: bfloat16 [4096, 2048], P(('tm', 'expert'))
- gate_weight_grad: float32 [32, 2048, 512], P(('tm', 'expert'))
- up_weight_grad: float32 [32, 2048, 512], P(('tm', 'expert'))
- down_weight_grad: float32 [32, 512, 2048], P(('tm', 'expert'))
Inputs may be any that keep to these rules, and one draw needn't show every extreme that they name: `expert_ids`: the two experts of a token differ.
All inputs are finite; a program needn't handle non-finite values.
Results may differ from a plain program's by a relative error of at most 0.017.
Values may be sent and summed in bfloat16 or wider, within the bound.
No kernel may reach another device: no remote copies, remote signals or barrier semaphores. Data moves between devices by JAX's collectives and lax.ppermute only.
A program may use at most 192 MiB of HBM per device.

v0:
```python
import jax
import jax.numpy as jnp
from jax import lax
from jax.sharding import PartitionSpec as P

HEADS = 16
HEAD_DIM = 128
SLICES = 4


epsilon = 1e-06
highest = lax.Precision.HIGHEST


def slot_places(routes, capacity, experts):
    flat_ids = routes.reshape(-1)
    onehot = (flat_ids[:, None] == jnp.arange(experts, dtype=jnp.int32)[None, :]).astype(jnp.int32)
    earlier = jnp.cumsum(onehot, axis=0) - onehot
    position = jnp.sum(earlier * onehot, axis=1)
    return jnp.where(position < capacity, flat_ids * capacity + position, experts * capacity)


def expert_slice(rows, grad_rows, gate_part, up_part, down_part):
    gate = jnp.dot(rows, gate_part, preferred_element_type=jnp.float32)
    upper = jnp.dot(rows, up_part, preferred_element_type=jnp.float32)
    sigma = jax.nn.sigmoid(gate)
    act = (gate * sigma * upper).astype(jnp.bfloat16)
    act_grad = jnp.dot(grad_rows, down_part.T, preferred_element_type=jnp.float32)
    down_grad = jnp.dot(act.T, grad_rows, preferred_element_type=jnp.float32)
    gate_grad = (act_grad * upper * sigma * (1.0 + gate * (1.0 - sigma))).astype(jnp.bfloat16)
    up_grad = (act_grad * gate * sigma).astype(jnp.bfloat16)
    gate_wgrad = jnp.dot(rows.T, gate_grad, preferred_element_type=jnp.float32)
    up_wgrad = jnp.dot(rows.T, up_grad, preferred_element_type=jnp.float32)
    partial_sum = jnp.dot(gate_grad, gate_part.T, preferred_element_type=jnp.float32)
    partial_sum = partial_sum + jnp.dot(up_grad, up_part.T, preferred_element_type=jnp.float32)
    return (partial_sum.astype(jnp.bfloat16), gate_wgrad, up_wgrad, down_grad)


def body(
    queries, keys, values, out_grad, expert_ids, combine_gates, gate_weight, up_weight, down_weight
):
    tok_rows = queries.shape[0]
    width = queries.shape[1]
    time_count = lax.axis_size("tm")
    group_count = lax.axis_size("expert")
    devices = time_count * group_count
    experts = devices // SLICES
    capacity = SLICES * max(1, 3 * tok_rows // (experts * SLICES))
    shape3 = (tok_rows, HEADS, HEAD_DIM)
    query_f = queries.astype(jnp.float32).reshape(shape3)
    key_f = keys.astype(jnp.float32).reshape(shape3)
    value_f = values.astype(jnp.float32).reshape(shape3)
    local = jnp.einsum("tha,thb->hab", key_f, value_f, precision=highest)
    everyone = lax.all_gather(local[None], "tm", axis=0, tiled=True)
    mine = lax.axis_index("tm")
    picks = (jnp.arange(everyone.shape[0], dtype=jnp.int32) <= mine).astype(jnp.float32)
    inclusive = jnp.einsum("c,chab->hab", picks, everyone, precision=highest)
    states = lax.psum(inclusive, "expert")
    mixed = jnp.einsum("tha,hab->thb", query_f, states, precision=highest)
    scale = lax.rsqrt(jnp.mean(mixed * mixed, axis=-1, keepdims=True) + epsilon)
    normed = mixed * scale
    hidden = normed.astype(jnp.bfloat16).reshape(tok_rows, width)
    places = slot_places(expert_ids, capacity, experts)
    rows_h = jnp.repeat(hidden, 2, axis=0)
    grad_f = out_grad.astype(jnp.float32)
    rows_g = (jnp.repeat(grad_f, 2, axis=0) * combine_gates.reshape(-1, 1)).astype(jnp.bfloat16)
    buffer_h = (
        jnp.zeros((experts * capacity, width), jnp.bfloat16).at[places].set(rows_h, mode="drop")
    )
    buffer_g = (
        jnp.zeros((experts * capacity, width), jnp.bfloat16).at[places].set(rows_g, mode="drop")
    )
    send_h = jnp.repeat(buffer_h.reshape(experts, capacity, width), SLICES, axis=0)
    send_g = jnp.repeat(buffer_g.reshape(experts, capacity, width), SLICES, axis=0)
    got_h, got_g = (
        lax.all_to_all(send_h, ("tm", "expert"), split_axis=0, concat_axis=0, tiled=True),
        lax.all_to_all(send_g, ("tm", "expert"), split_axis=0, concat_axis=0, tiled=True),
    )
    got_h = got_h.reshape(1, devices, capacity, width)
    got_g = got_g.reshape(1, devices, capacity, width)
    rows = got_h.reshape(-1, width)
    grad_rows = got_g.reshape(-1, width)
    partial_sum, gate_wgrad, up_wgrad, down_grad = expert_slice(
        rows, grad_rows, gate_weight[0], up_weight[0], down_weight[0]
    )
    payload = partial_sum.astype(jnp.float32).reshape(devices, capacity, width)
    returned = lax.all_to_all(
        payload.astype(jnp.bfloat16), ("tm", "expert"), split_axis=0, concat_axis=0, tiled=True
    ).astype(payload.dtype)
    summed = jnp.sum(returned.reshape(experts, SLICES, capacity, width), axis=1)
    per_choice = jnp.take(
        summed.reshape(experts * capacity, width), places, axis=0, mode="fill", fill_value=0.0
    )
    moe_grad = jnp.sum(per_choice.reshape(tok_rows, 2, width), axis=1)
    hidden_grad = (grad_f + moe_grad).reshape(shape3)
    norm_grad = scale * (
        hidden_grad - normed * jnp.mean(hidden_grad * normed, axis=-1, keepdims=True)
    )
    query_grad = jnp.einsum("thb,hab->tha", norm_grad, states, precision=highest)
    local_back = jnp.einsum("tha,thb->hab", query_f, norm_grad, precision=highest)
    every_back = lax.all_gather(
        local_back[None].astype(jnp.bfloat16), "tm", axis=0, tiled=True
    ).astype(jnp.float32)
    mine_back = lax.axis_index("tm")
    picks_back = (jnp.arange(every_back.shape[0], dtype=jnp.int32) >= mine_back).astype(jnp.float32)
    inclusive_back = jnp.einsum("c,chab->hab", picks_back, every_back, precision=highest)
    back_states = lax.psum(inclusive_back.astype(jnp.bfloat16), "expert").astype(jnp.float32)
    key_grad = jnp.einsum("thb,hab->tha", value_f, back_states, precision=highest)
    value_grad = jnp.einsum("tha,hab->thb", key_f, back_states, precision=highest)
    return (
        query_grad.reshape(tok_rows, width).astype(jnp.bfloat16),
        key_grad.reshape(tok_rows, width).astype(jnp.bfloat16),
        value_grad.reshape(tok_rows, width).astype(jnp.bfloat16),
        gate_wgrad[None],
        up_wgrad[None],
        down_grad[None],
    )


def solution(mesh):
    placed = (
        P(("tm", "expert"), None),
        P(("tm", "expert"), None),
        P(("tm", "expert"), None),
        P(("tm", "expert"), None),
        P(("tm", "expert"), None),
        P(("tm", "expert"), None),
        P(("tm", "expert"), None, None),
        P(("tm", "expert"), None, None),
        P(("tm", "expert"), None, None),
    )
    return jax.shard_map(
        body,
        mesh=mesh,
        in_specs=placed,
        out_specs=(
            P(("tm", "expert"), None),
            P(("tm", "expert"), None),
            P(("tm", "expert"), None),
            P(("tm", "expert"), None, None),
            P(("tm", "expert"), None, None),
            P(("tm", "expert"), None, None),
        ),
        check_vma=False,
    )
```

profile of v0, /device:TPU:0, one launch (start us, length us, event | category | flops | bytes accessed | tf_op | source)
XLA Modules:
  0.0 743.5 jit_solution(12037618566294327427)
XLA Ops:
  7.2 2.7 fusion.23
  10.0 37.4 %all-gather.5.cloned.1.call-done = f32[64,128,128]{2,1,0:T(8,128)} async-done(((f32[16,128,128]{2,1,0:T(8,128)}), f32[64,128,128]{2,1,0:T(8,128)}) %all-gather.5.cloned.1.call-update) | async-done | bytes 4194320 | tf_op jit(solution)/shard_map/all_gather | solution.py:54
  47.3 8.5 %fusion = f32[1,16,128,128]{3,0,2,1:T(1,128)S(1)} fusion(f32[4,16,128,128]{3,2,1,0:T(8,128)} %bitcast.135, s32[]{:T(128)S(6)} %axis_index.19), kind=kOutput, calls=%fused_computation.5 | convolution fusion | flops 12582916 | bytes 5242884 | tf_op jit(solution)/shard_map/c,chab->hab/dot_general | solution.py:57
  59.3 76.9 %all-reduce.3.cloned.1.call-done = f32[16,128,128]{1,2,0:T(8,128)} async-done(((f32[16,128,128]{1,2,0:T(8,128)}), f32[16,128,128]{1,2,0:T(8,128)}) %all-reduce.3.cloned.1.call-update) | async-done | bytes 1048592 | tf_op jit(solution)/shard_map/psum | solution.py:58
  136.2 2.6 multiply_reduce_fusion.1
  143.8 4.4 scatter_custom_fusion.1
  148.2 4.9 broadcast_in_dim.53
  153.1 4.3 all-to-all-start.1
  157.7 2.4 broadcast_in_dim.50
  160.1 3.6 reshape.147
  163.7 4.5 scatter_custom_fusion
  168.3 129.2 %all-to-all-done.1 = bf16[32,48,2048]{2,1,0:T(8,128)(2,1)} async-done(((bf16[32,48,2048]{2,1,0:T(8,128)(2,1)}), bf16[32,48,2048]{2,1,0:T(8,128)(2,1)}, u32[]{:S(2)}, u32[]{:S(2)}) %all-to-all-start.1) | async-done | bytes 6291488 | tf_op jit(solution)/shard_map/all_to_all | solution.py:76
  297.4 4.9 broadcast_in_dim.51
  302.3 3.6 all-to-all-start
  306.0 8.0 %fusion.4 = f32[1536,512]{1,0:T(8,128)} fusion(bf16[1536,2048]{1,0:T(8,128)(2,1)} %bitcast.16, bf16[1,2048,512]{2,1,0:T(8,128)(2,1)S(1)} %copy-done), kind=kOutput, calls=%fused_computation.16 | convolution fusion | flops 3221225472 | bytes 11534336 | tf_op jit(solution)/shard_map/dot_general | solution.py:24
  314.0 7.9 %fusion.7 = f32[1536,512]{1,0:T(8,128)} fusion(bf16[1536,2048]{1,0:T(8,128)(2,1)} %bitcast.16, bf16[1,2048,512]{2,1,0:T(8,128)(2,1)S(1)} %copy-done.10), kind=kOutput, calls=%fused_computation.19 | convolution fusion | flops 3221225472 | bytes 11534336 | tf_op jit(solution)/shard_map/dot_general | solution.py:25
  321.9 124.0 %all-to-all-done = bf16[32,48,2048]{2,1,0:T(8,128)(2,1)} async-done(((bf16[32,48,2048]{2,1,0:T(8,128)(2,1)}), bf16[32,48,2048]{2,1,0:T(8,128)(2,1)}, u32[]{:S(2)}, u32[]{:S(2)}) %all-to-all-start) | async-done | bytes 6291488 | tf_op jit(solution)/shard_map/all_to_all | solution.py:77
  445.9 9.8 %multiply_convert_fusion.1 = (bf16[1536,512]{1,0:T(8,128)(2,1)S(1)}, bf16[1536,512]{1,0:T(8,128)(2,1)S(1)}) fusion(f32[1536,512]{1,0:T(8,128)} %fusion.4, f32[1536,512]{1,0:T(8,128)} %fusion.7, bf16[1536,2048]{1,0:T(8,128)(2,1)} %bitcast.11, bf16[1,512,2048]{2,1,0:T(8,128)(2,1)} %param.17), kind=kOutput, calls=%fused_computation.11 | convolution fusion | flops 3231449088 | bytes 17825792 | tf_op jit(solution)/shard_map/dot_general | solution.py:28
  455.8 6.5 fusion.2
  462.3 8.5 %add_convert_fusion = bf16[1536,2048]{1,0:T(8,128)(2,1)} fusion(f32[1536,2048]{1,0:T(8,128)} %fusion.2, bf16[1536,512]{1,0:T(8,128)(2,1)S(1)} %get-tuple-element.24, bf16[1,2048,512]{2,1,0:T(8,128)(2,1)S(1)} %copy-done.11), kind=kOutput, calls=%fused_computation.4 | convolution fusion | flops 3227516928 | bytes 22544384 | tf_op jit(solution)/shard_map/dot_general | solution.py:35
  470.8 3.6 all-to-all-start.2
  474.6 139.8 %all-to-all-done.2 = bf16[32,48,2048]{2,1,0:T(8,128)(2,1)} async-done(((bf16[32,48,2048]{2,1,0:T(8,128)(2,1)}), bf16[32,48,2048]{2,1,0:T(8,128)(2,1)}, u32[]{:S(2)}, u32[]{:S(2)}) %all-to-all-start.2) | async-done | bytes 6291488 | tf_op jit(solution)/shard_map/all_to_all | solution.py:87
  614.4 4.4 convert_reduce_fusion
  618.8 2.7 gather_fusion
  621.5 2.5 gather.7
  624.0 4.5 select_reduce_fusion
  633.0 8.9 %convolution_bitcast_fusion.1 = f32[1,2048,512]{2,1,0:T(8,128)} fusion(bf16[1536,2048]{1,0:T(8,128)(2,1)} %bitcast.16, bf16[1536,512]{1,0:T(8,128)(2,1)} %copy-done.12), kind=kOutput, calls=%fused_computation.8 | convolution fusion | flops 3221225472 | bytes 12058624 | tf_op jit(solution)/shard_map/dot_general | solution.py:33
  641.9 8.1 %convolution_bitcast_fusion = f32[1,512,2048]{2,1,0:T(8,128)} fusion(bf16[1536,2048]{1,0:T(8,128)(2,1)} %bitcast.11, f32[1536,512]{1,0:T(8,128)S(1)} %copy-done.15, f32[1536,512]{1,0:T(8,128)S(1)} %copy-done.14), kind=kOutput, calls=%fused_computation.7 | convolution fusion | flops 3225944064 | bytes 16777216 | tf_op jit(solution)/shard_map/dot_general | solution.py:29
  650.0 4.3 all-gather.7.cloned.1.call-done
  654.2 3.3 fusion.11
  658.5 8.8 %convolution_bitcast_fusion.2 = f32[1,2048,512]{2,1,0:T(8,128)} fusion(bf16[1536,2048]{1,0:T(8,128)(2,1)} %bitcast.16, bf16[1536,512]{1,0:T(8,128)(2,1)} %copy-done.13), kind=kOutput, calls=%fused_computation.9 | convolution fusion | flops 3221225472 | bytes 12058624 | tf_op jit(solution)/shard_map/dot_general | solution.py:32
  670.3 61.0 %all-reduce.5.cloned.1.call-done = bf16[16,128,128]{2,1,0:T(8,128)(2,1)} async-done(((bf16[16,128,128]{2,1,0:T(8,128)(2,1)}), bf16[16,128,128]{2,1,0:T(8,128)(2,1)}) %all-reduce.5.cloned.1.call-update) | async-done | bytes 524304 | tf_op jit(solution)/shard_map/psum | solution.py:107
  (76 shorter events, 22.6 us)
Async XLA Ops:
  7.2 298.8 %copy-start = (bf16[1,2048,512]{2,1,0:T(8,128)(2,1)S(1)}, bf16[1,2048,512]{2,1,0:T(8,128)(2,1)}, u32[]{:S(2)}) copy-start(bf16[1,2048,512]{2,1,0:T(8,128)(2,1)} %param.15) | copy-start | bytes 6291460
  7.2 40.2 %all-gather.5.cloned.1.call-start = ((), (), s32[]{:S(2)}) async-start(), calls=%async_computation.5 | async-start | bytes 5242880 | tf_op jit(solution)/shard_map/all_gather | solution.py:54
  9.9 126.3 %all-reduce.3.cloned.1.call-start = ((), (), s32[]{:S(2)}) async-start(), calls=%async_computation.3 | async-start | bytes 2097152 | tf_op jit(solution)/shard_map/psum | solution.py:58
  47.3 10.5 %copy-start.8 = (s32[128,2]{0,1:T(2,128)S(1)}, s32[128,2]{0,1:T(2,128)}, u32[]{:S(2)}) copy-start(s32[128,2]{0,1:T(2,128)} %param.13) | copy-start | bytes 3076
  138.8 1.0 copy-start.2
  153.1 4.3 copy-start.9
  153.1 4.6 copy-start.5
  153.1 144.3 %all-to-all-start.1 = ((bf16[32,48,2048]{2,1,0:T(8,128)(2,1)}), bf16[32,48,2048]{2,1,0:T(8,128)(2,1)}, u32[]{:S(2)}, u32[]{:S(2)}) async-start(bf16[32,48,2048]{2,1,0:T(8,128)(2,1)} %bitcast.128), calls=%async_computation.1 | async-start | bytes 12582912 | tf_op jit(solution)/shard_map/all_to_all | solution.py:76
  302.3 143.6 %all-to-all-start = ((bf16[32,48,2048]{2,1,0:T(8,128)(2,1)}), bf16[32,48,2048]{2,1,0:T(8,128)(2,1)}, u32[]{:S(2)}, u32[]{:S(2)}) async-start(bf16[32,48,2048]{2,1,0:T(8,128)(2,1)} %bitcast.129), calls=%async_computation | async-start | bytes 12582912 | tf_op jit(solution)/shard_map/all_to_all | solution.py:77
  305.9 8.1 %copy-start.10 = (bf16[1,2048,512]{2,1,0:T(8,128)(2,1)S(1)}, bf16[1,2048,512]{2,1,0:T(8,128)(2,1)}, u32[]{:S(2)}) copy-start(bf16[1,2048,512]{2,1,0:T(8,128)(2,1)} %param.16) | copy-start | bytes 6291460
  455.7 6.5 copy-start.13
  455.8 6.5 copy-start.12
  455.8 6.5 copy-start.11
  470.8 143.6 %all-to-all-start.2 = ((bf16[32,48,2048]{2,1,0:T(8,128)(2,1)}), bf16[32,48,2048]{2,1,0:T(8,128)(2,1)}, u32[]{:S(2)}, u32[]{:S(2)}) async-start(bf16[32,48,2048]{2,1,0:T(8,128)(2,1)} %bitcast.132), calls=%async_computation.2 | async-start | bytes 12582912 | tf_op jit(solution)/shard_map/all_to_all | solution.py:87
  474.4 179.8 %all-gather.7.cloned.1.call-start = ((), (), s32[]{:S(2)}) async-start(), calls=%async_computation.6 | async-start | bytes 2621440 | tf_op jit(solution)/shard_map/all_gather | solution.py:101
  624.0 4.5 copy-start.6
  628.5 1.2 copy-start.3
  632.7 98.6 %all-reduce.5.cloned.1.call-start = ((), (), s32[]{:S(2)}) async-start(), calls=%async_computation.4 | async-start | bytes 1048576 | tf_op jit(solution)/shard_map/psum | solution.py:107
  633.0 8.9 %copy-start.14 = (f32[1536,512]{1,0:T(8,128)S(1)}, f32[1536,512]{1,0:T(8,128)}, u32[]{:S(2)}) copy-start(f32[1536,512]{1,0:T(8,128)} %fusion.4) | copy-start | bytes 9437188
  633.0 8.9 %copy-start.15 = (f32[1536,512]{1,0:T(8,128)S(1)}, f32[1536,512]{1,0:T(8,128)}, u32[]{:S(2)}) copy-start(f32[1536,512]{1,0:T(8,128)} %fusion.7) | copy-start | bytes 9437188
  658.4 8.8 %copy-start.4 = (f32[16,128,128]{1,2,0:T(8,128)S(1)}, f32[16,128,128]{1,2,0:T(8,128)}, u32[]{:S(2)}) copy-start(f32[16,128,128]{1,2,0:T(8,128)} %all-reduce.3.cloned.1.call-done) | copy-start | bytes 3145732
  667.2 64.0 %copy-start.7 = (bf16[128,2048]{1,0:T(8,128)(2,1)S(1)}, bf16[128,2048]{1,0:T(8,128)(2,1)}, u32[]{:S(2)}) copy-start(bf16[128,2048]{1,0:T(8,128)(2,1)} %param.11) | copy-start | bytes 1572868
  669.2 67.3 %copy-start.1 = (bf16[1,2048,512]{2,1,0:T(8,128)(2,1)S(1)}, bf16[1,2048,512]{2,1,0:T(8,128)(2,1)}, u32[]{:S(2)}) copy-start(bf16[1,2048,512]{2,1,0:T(8,128)(2,1)} %param.15) | copy-start | bytes 6291460
Sparse Core Ops, SparseCore 0:
  10.1 37.1 all-gather.4
  57.9 78.2 all-reduce.2
  632.8 21.3 all-gather.6
  658.6 72.6 all-reduce.4
where the time goes:
time: 753 us; the launch traced here: 743 us
  waiting for transfers between devices  573 us (76%)
  matrix products  90.6 us (12%)
  local copies, waits for them, and re-layouts  38.4 us (5%)
  other arithmetic  15.5 us (2%)
  between operations  14.5 us (2%)
  starting transfers between devices  11.9 us (2%)
    all_to_all x1, waiting for transfers between devices, body(): lax.all_to_all(payload.astype(jnp.bfloat16), ('tm', 'expert'), split_axis...  140 us
    all_to_all x1, waiting for transfers between devices, body(): lax.all_to_all(send_h, ('tm', 'expert'), split_axis=0, concat_axis=0, til...  129 us
    all_to_all x1, waiting for transfers between devices, body(): lax.all_to_all(send_g, ('tm', 'expert'), split_axis=0, concat_axis=0, til...  124 us
    psum x1, waiting for transfers between devices, body(): states = lax.psum(inclusive, 'expert')  76.9 us
    psum x1, waiting for transfers between devices, body(): lax.psum(inclusive_back.astype(jnp.bfloat16), 'expert').astype(jnp.float32)  61 us
    all_gather x1, waiting for transfers between devices, body(): everyone = lax.all_gather(local[None], 'tm', axis=0, tiled=True)  37.4 us
  transfers between devices with their start and end apart: 7, of which 7 were waited for; matrix products, arithmetic and copies ran while one was open for 8% of the time, Pallas kernels for 0%

commit v1 on v0

v1 whole, which is shorter than its diff:
```python
import functools

import jax
import jax.numpy as jnp
from jax import lax
from jax.experimental import pallas as pl
from jax.experimental.pallas import tpu as pltpu
from jax.sharding import Mesh, PartitionSpec as P

HEADS = 16
HEAD_DIM = 128
SLICES = 4
EPSILON = 1e-06
ALL = ("tm", "eg", "sl")
F32 = jnp.float32
BF16 = jnp.bfloat16


def dot(a, b):
    return jnp.dot(a, b, preferred_element_type=F32)


def dot_nt(a, b):
    return lax.dot_general(a, b, (((1,), (1,)), ((), ())), preferred_element_type=F32)


def dot_tn(a, b):
    return lax.dot_general(a, b, (((0,), (0,)), ((), ())), preferred_element_type=F32)


def slot_places(routes, capacity, experts):
    flat_ids = routes.reshape(-1)
    onehot = (flat_ids[:, None] == jnp.arange(experts, dtype=jnp.int32)[None, :]).astype(jnp.int32)
    earlier = jnp.cumsum(onehot, axis=0) - onehot
    position = jnp.sum(earlier * onehot, axis=1)
    return jnp.where(position < capacity, flat_ids * capacity + position, experts * capacity)


def swap(value, bit):
    return lax.ppermute(value, "sl", [(i, i ^ bit) for i in range(SLICES)])


def exchange(value, axes):
    return lax.all_to_all(value, axes, split_axis=0, concat_axis=0, tiled=True)


def spread(rows):
    half = rows.shape[0] // 2
    a, b = rows[:half], rows[half:]
    ax, bz = swap(a, 1), swap(b, 2)
    az, bx = swap(a, 2), swap(b, 1)
    ad, bd = swap(ax, 2), swap(bz, 1)
    return (a, b), (ax, bx), (az, bz), (ad, bd)


def wgrad_kernel(count, *refs):
    xs, ys, acts, ggs, ugs = (refs[i * count : (i + 1) * count] for i in range(5))
    gate_out, up_out, down_out = refs[5 * count :]
    gate = up = down = None
    for x, y, act, gg, ug in zip(xs, ys, acts, ggs, ugs):
        g, u, d = dot_tn(x[...], gg[...]), dot_tn(x[...], ug[...]), dot_tn(act[...], y[...])
        gate = g if gate is None else gate + g
        up = u if up is None else up + u
        down = d if down is None else down + d
    gate_out[...], up_out[...], down_out[...] = gate, up, down


def weight_grads(xs, ys, acts, ggs, ugs):
    width = xs[0].shape[1]
    hidden = acts[0].shape[1]
    block = min(256, width)
    wide = [pl.BlockSpec((x.shape[0], block), lambda i: (0, i)) for x in xs]
    full = [pl.BlockSpec((x.shape[0], hidden), lambda i: (0, 0)) for x in xs]
    return pl.pallas_call(
        functools.partial(wgrad_kernel, len(xs)),
        grid=(width // block,),
        in_specs=wide + wide + full + full + full,
        out_specs=[
            pl.BlockSpec((block, hidden), lambda i: (i, 0)),
            pl.BlockSpec((block, hidden), lambda i: (i, 0)),
            pl.BlockSpec((hidden, block), lambda i: (0, i)),
        ],
        out_shape=[
            jax.ShapeDtypeStruct((width, hidden), F32),
            jax.ShapeDtypeStruct((width, hidden), F32),
            jax.ShapeDtypeStruct((hidden, width), F32),
        ],
        name="weight_grads",
    )(*xs, *ys, *acts, *ggs, *ugs)


def body(queries, keys, values, out_grad, expert_ids, combine_gates, gate_weight, up_weight, down_weight):
    tok_rows, width = queries.shape
    times, groups = lax.axis_size("tm"), lax.axis_size("eg")
    experts = times * groups
    devices = experts * SLICES
    per_span = groups * SLICES
    capacity = SLICES * max(1, 3 * tok_rows // (experts * SLICES))
    shape3 = (tok_rows, HEADS, HEAD_DIM)
    state_rows = HEADS * HEAD_DIM // devices
    gate_w, up_w, down_w = gate_weight[0], up_weight[0], down_weight[0]
    query3, key3, value3 = queries.reshape(shape3), keys.reshape(shape3), values.reshape(shape3)

    def span_sums(terms, backward):
        got = exchange(terms.astype(BF16).reshape(HEADS * HEAD_DIM, HEAD_DIM), ALL)
        got = got.reshape(times, per_span, state_rows, HEAD_DIM).astype(F32)
        spans = jnp.sum(got, axis=1)
        order = range(times - 1, -1, -1) if backward else range(times)
        total, sums = None, [None] * times
        for c in order:
            total = spans[c] if total is None else total + spans[c]
            sums[c] = total
        sums = jnp.stack(sums).astype(BF16)
        send = jnp.broadcast_to(sums[:, None], (times, per_span, state_rows, HEAD_DIM))
        back = exchange(send.reshape(devices * state_rows, HEAD_DIM), ALL)
        return back.reshape(HEADS, HEAD_DIM, HEAD_DIM)

    places = slot_places(expert_ids, capacity, experts).reshape(tok_rows, 2)
    slots = jnp.arange(experts * capacity, dtype=jnp.int32)
    pick = [(slots[:, None] == places[None, :, k]).astype(BF16) for k in range(2)]
    pick_both = jnp.concatenate(pick, axis=1)
    pick_token = pick[0] + pick[1]

    local = jnp.einsum("tha,thb->hab", key3, value3, preferred_element_type=F32)
    states = span_sums(local, False)

    grad_f = out_grad.astype(F32)
    scaled = jnp.concatenate([(grad_f * combine_gates[:, k : k + 1]).astype(BF16) for k in range(2)])
    slot_g = dot(pick_both, scaled).astype(BF16)
    grads = spread(exchange(slot_g, ("tm", "eg")))

    mixed = jnp.einsum("tha,hab->thb", query3, states, preferred_element_type=F32)
    scale = lax.rsqrt(jnp.mean(mixed * mixed, axis=-1, keepdims=True) + EPSILON)
    normed = mixed * scale
    hidden = normed.astype(BF16).reshape(tok_rows, width)
    slot_h = dot(pick_token, hidden).astype(BF16)
    rows = spread(exchange(slot_h, ("tm", "eg")))

    flat = lambda nested: [piece for pair in nested for piece in pair]
    xs, ys = flat(rows), flat(grads)
    acts, ggs, ugs, parts = [], [], [], []
    for x, y in zip(xs, ys):
        gate, upper = dot(x, gate_w), dot(x, up_w)
        sigma = jax.nn.sigmoid(gate)
        act_grad = dot_nt(y, down_w)
        acts.append((gate * sigma * upper).astype(BF16))
        gg = (act_grad * upper * sigma * (1.0 + gate * (1.0 - sigma))).astype(BF16)
        ug = (act_grad * gate * sigma).astype(BF16)
        ggs.append(gg)
        ugs.append(ug)
        parts.append(dot_nt(gg, gate_w) + dot_nt(ug, up_w))
    (oa, ob, xa, xb, za, zb, da, db) = parts
    da_in, db_in = swap(da.astype(BF16), 2), swap(db.astype(BF16), 1)
    za_in, xb_in = swap(za.astype(BF16), 2), swap(xb.astype(BF16), 1)
    xa_in = swap((xa + da_in.astype(F32)).astype(BF16), 1)
    zb_in = swap((zb + db_in.astype(F32)).astype(BF16), 2)
    own = jnp.concatenate(
        [
            (oa + za_in.astype(F32) + xa_in.astype(F32)).astype(BF16),
            (ob + xb_in.astype(F32) + zb_in.astype(F32)).astype(BF16),
        ]
    )
    gate_wgrad, up_wgrad, down_grad = weight_grads(xs, ys, acts, ggs, ugs)
    returned = exchange(own, ("tm", "eg"))
    moe_grad = dot_tn(pick_token, returned)
    hidden_grad = (grad_f + moe_grad).reshape(shape3)
    norm_grad = scale * (hidden_grad - normed * jnp.mean(hidden_grad * normed, axis=-1, keepdims=True))
    norm_grad = norm_grad.astype(BF16)
    local_back = jnp.einsum("tha,thb->hab", query3, norm_grad, preferred_element_type=F32)
    back_states = span_sums(local_back, True)
    query_grad = jnp.einsum("thb,hab->tha", norm_grad, states, preferred_element_type=F32)
    key_grad = jnp.einsum("thb,hab->tha", value3, back_states, preferred_element_type=F32)
    value_grad = jnp.einsum("tha,hab->thb", key3, back_states, preferred_element_type=F32)
    return (
        query_grad.reshape(tok_rows, width).astype(BF16),
        key_grad.reshape(tok_rows, width).astype(BF16),
        value_grad.reshape(tok_rows, width).astype(BF16),
        gate_wgrad[None],
        up_wgrad[None],
        down_grad[None],
    )


def solution(mesh):
    times, members = mesh.devices.shape
    fine = Mesh(mesh.devices.reshape(times, members // SLICES, SLICES), ALL)
    two, three = P(ALL, None), P(ALL, None, None)
    return jax.shard_map(
        body,
        mesh=fine,
        in_specs=(two,) * 6 + (three,) * 3,
        out_specs=(two,) * 3 + (three,) * 3,
        check_vma=False,
    )
```

time: 753 us -> 402 us (0.53); the launches traced: 743 us -> 401 us
  waiting for transfers between devices: 573 us -> 203 us
  blocking collectives: 0 us -> 60 us
  matrix products: 90.6 us -> 57.1 us
  starting transfers between devices: 11.9 us -> 38.1 us
  local copies, waits for them, and re-layouts: 38.4 us -> 17.4 us
  Pallas kernels: 0 us -> 19.8 us
  between operations: 14.5 us -> 1.41 us
  other arithmetic: 15.5 us -> 3.92 us
    all_to_all x3 -> x5, waiting for transfers between devices: 393 us -> 62.5 us  [exchange(): return lax.all_to_all(value, axes, split_axis=0, concat_axis=0, tiled=True)]
    ppermute x0 -> x18, waiting for transfers between devices: none -> 141 us  [swap(): return lax.ppermute(value, 'sl', [(i, i ^ bit) for i in range(SLICES)])]
    psum x2 -> x0, waiting for transfers between devices: 138 us -> none  [the longest x1 76.9 us: body(): states = lax.psum(inclusive, 'expert')]
    all_to_all x0 -> x2, blocking collectives: none -> 60 us  [exchange(): return lax.all_to_all(value, axes, split_axis=0, concat_axis=0, tiled=True)]
    all_gather x2 -> x0, waiting for transfers between devices: 41.6 us -> none  [the longest x1 37.4 us: body(): everyone = lax.all_gather(local[None], 'tm', axis=0, tiled=True)]
    dot_general x16 -> x49, matrix products: 90.6 us -> 57.1 us  [the longest x24 26.2 us: dot_nt(): lax.dot_general(a, b, (((1,), (1,)), ((), ())), preferred_element_type=F32)]
    pallas_call x0 -> x1, Pallas kernels: none -> 19.8 us  [weight_grads(): pl.pallas_call(functools.partial(wgrad_kernel, len(xs)), grid=(width // b...]
    ppermute x0 -> x18, starting transfers between devices: none -> 16.7 us  [swap(): return lax.ppermute(value, 'sl', [(i, i ^ bit) for i in range(SLICES)])]
  transfers between devices with their start and end apart: 7 -> 23, of which waited for: 7 -> 13; matrix products, arithmetic and copies ran while one was open for 8% -> 14% of each run, Pallas kernels for 0% -> 5%
where the time goes in v1:
time: 402 us; the launch traced here: 401 us
  waiting for transfers between devices  203 us (50%)
  blocking collectives  60 us (15%)
  matrix products  57.1 us (14%)
  starting transfers between devices  38.1 us (9%)
  Pallas kernels  19.8 us (5%)
  local copies, waits for them, and re-layouts  17.4 us (4%)
    ppermute x18, waiting for transfers between devices, swap(): return lax.ppermute(value, 'sl', [(i, i ^ bit) for i in range(SLICES)])  141 us
    all_to_all x5, waiting for transfers between devices, exchange(): return lax.all_to_all(value, axes, split_axis=0, concat_axis=0, tiled=True)  62.5 us
    all_to_all x2, blocking collectives, exchange(): return lax.all_to_all(value, axes, split_axis=0, concat_axis=0, tiled=True)  60 us
    dot_general x24, matrix products, dot_nt(): lax.dot_general(a, b, (((1,), (1,)), ((), ())), preferred_element_type=F32)  26.2 us
    all_to_all x5, starting transfers between devices, exchange(): return lax.all_to_all(value, axes, split_axis=0, concat_axis=0, tiled=True)  21.3 us
    pallas_call x1, Pallas kernels, weight_grads(): pl.pallas_call(functools.partial(wgrad_kernel, len(xs)), grid=(width // b...  19.8 us
    dot_general x18, matrix products, dot(): return jnp.dot(a, b, preferred_element_type=F32)  19.1 us
    ppermute x18, starting transfers between devices, swap(): return lax.ppermute(value, 'sl', [(i, i ^ bit) for i in range(SLICES)])  16.7 us
  transfers between devices with their start and end apart: 23, of which 13 were waited for; matrix products, arithmetic and copies ran while one was open for 14% of the time, Pallas kernels for 5%

profile of v1, /device:TPU:0, one launch (start us, length us, event | category | flops | bytes accessed | tf_op | source)
XLA Modules:
  0.0 401.0 jit_solution(3388799245469931169)
XLA Ops:
  0.7 2.5 convolution_convert_fusion.6
  3.2 7.3 %all-to-all-start = ((bf16[32,64,128]{2,1,0:T(8,128)(2,1)}), bf16[32,64,128]{2,1,0:T(8,128)(2,1)S(1)}, u32[]{:S(2)}, u32[]{:S(2)}) async-start(bf16[32,64,128]{2,1,0:T(8,128)(2,1)} %bitcast), calls=%async_computation | async-start | bytes 1048576 | tf_op jit(solution)/shard_map/all_to_all | solution.py:44
  12.1 14.6 %all-to-all-done = bf16[32,64,128]{2,1,0:T(8,128)(2,1)S(1)} async-done(((bf16[32,64,128]{2,1,0:T(8,128)(2,1)}), bf16[32,64,128]{2,1,0:T(8,128)(2,1)S(1)}, u32[]{:S(2)}, u32[]{:S(2)}) %all-to-all-start) | async-done | bytes 524320 | tf_op jit(solution)/shard_map/all_to_all | solution.py:44
  27.8 2.6 all-to-all-start.1
  32.6 14.0 %all-to-all-done.1 = bf16[32,64,128]{2,1,0:T(8,128)(2,1)S(1)} async-done(((bf16[32,64,128]{2,1,0:T(8,128)(2,1)}), bf16[32,64,128]{2,1,0:T(8,128)(2,1)S(1)}, u32[]{:S(2)}, u32[]{:S(2)}) %all-to-all-start.1) | async-done | bytes 524320 | tf_op jit(solution)/shard_map/all_to_all | solution.py:44
  46.6 4.3 %all-to-all-start.2 = ((bf16[8,48,2048]{2,1,0:T(8,128)(2,1)}), bf16[8,48,2048]{2,1,0:T(8,128)(2,1)}, u32[]{:S(2)}, u32[]{:S(2)}) async-start(bf16[8,48,2048]{2,1,0:T(8,128)(2,1)} %bitcast.262), calls=%async_computation.2 | async-start | bytes 3145728 | tf_op jit(solution)/shard_map/all_to_all | solution.py:44
  55.4 33.9 %all-to-all-done.2 = bf16[8,48,2048]{2,1,0:T(8,128)(2,1)} async-done(((bf16[8,48,2048]{2,1,0:T(8,128)(2,1)}), bf16[8,48,2048]{2,1,0:T(8,128)(2,1)}, u32[]{:S(2)}, u32[]{:S(2)}) %all-to-all-start.2) | async-done | bytes 1572896 | tf_op jit(solution)/shard_map/all_to_all | solution.py:44
  89.3 4.5 %all-to-all-start.3 = ((bf16[8,48,2048]{2,1,0:T(8,128)(2,1)}), bf16[8,48,2048]{2,1,0:T(8,128)(2,1)}, u32[]{:S(2)}, u32[]{:S(2)}) async-start(bf16[8,48,2048]{2,1,0:T(8,128)(2,1)} %bitcast.250), calls=%async_computation.3 | async-start | bytes 3145728 | tf_op jit(solution)/shard_map/all_to_all | solution.py:44
  95.8 1.9 collective-permute-start.9
  97.7 1.9 collective-permute-start
  102.9 29.9 %collective-permute-done.12.refs_13_ = bf16[192,2048]{1,0:T(8,128)(2,1)S(1)} collective-permute-done((bf16[192,2048]{1,0:T(8,128)(2,1)S(1)}, bf16[192,2048]{1,0:T(8,128)(2,1)S(1)}, u32[]{:S(2)}, u32[]{:S(2)}) %collective-permute-start.12) | collective-permute-done | bytes 786464 | tf_op jit(solution)/shard_map/ppermute | solution.py:40
  137.7 11.9 %collective-permute-done.refs_12_ = bf16[192,2048]{1,0:T(8,128)(2,1)S(1)} collective-permute-done((bf16[192,2048]{1,0:T(8,128)(2,1)S(1)}, bf16[192,2048]{1,0:T(8,128)(2,1)S(1)}, u32[]{:S(2)}, u32[]{:S(2)}) %collective-permute-start) | collective-permute-done | bytes 786464 | tf_op jit(solution)/shard_map/ppermute | solution.py:40
  152.8 12.9 %collective-permute-done.5.refs_14_ = bf16[192,2048]{1,0:T(8,128)(2,1)S(1)} collective-permute-done((bf16[192,2048]{1,0:T(8,128)(2,1)S(1)}, bf16[192,2048]{1,0:T(8,128)(2,1)S(1)}, u32[]{:S(2)}, u32[]{:S(2)}) %collective-permute-start.5) | collective-permute-done | bytes 786464 | tf_op jit(solution)/shard_map/ppermute | solution.py:40
  173.3 2.0 collective-permute-start.1
  180.6 9.8 %collective-permute-done.10.refs_3_ = bf16[192,2048]{1,0:T(8,128)(2,1)S(1)} collective-permute-done((bf16[192,2048]{1,0:T(8,128)(2,1)S(1)}, bf16[192,2048]{1,0:T(8,128)(2,1)S(1)}, u32[]{:S(2)}, u32[]{:S(2)}) %collective-permute-start.10) | collective-permute-done | bytes 786464 | tf_op jit(solution)/shard_map/ppermute | solution.py:40
  194.3 1.9 collective-permute-start.15
  196.2 9.4 %collective-permute-done.1.refs_4_ = bf16[192,2048]{1,0:T(8,128)(2,1)S(1)} collective-permute-done((bf16[192,2048]{1,0:T(8,128)(2,1)S(1)}, bf16[192,2048]{1,0:T(8,128)(2,1)S(1)}, u32[]{:S(2)}, u32[]{:S(2)}) %collective-permute-start.1) | collective-permute-done | bytes 786464 | tf_op jit(solution)/shard_map/ppermute | solution.py:40
  214.0 25.4 %collective-permute-done.15.refs_7_ = bf16[192,2048]{1,0:T(8,128)(2,1)S(1)} collective-permute-done((bf16[192,2048]{1,0:T(8,128)(2,1)S(1)}, bf16[192,2048]{1,0:T(8,128)(2,1)S(1)}, u32[]{:S(2)}, u32[]{:S(2)}) %collective-permute-start.15) | collective-permute-done | bytes 786464 | tf_op jit(solution)/shard_map/ppermute | solution.py:40
  249.7 11.4 %collective-permute-done.16 = bf16[192,2048]{1,0:T(8,128)(2,1)S(1)} collective-permute-done((bf16[192,2048]{1,0:T(8,128)(2,1)S(1)}, bf16[192,2048]{1,0:T(8,128)(2,1)S(1)}, u32[]{:S(2)}, u32[]{:S(2)}) %collective-permute-start.16) | collective-permute-done | bytes 786464 | tf_op jit(solution)/shard_map/ppermute | solution.py:40
  264.9 2.7 collective-permute-done.7
  271.0 13.4 %collective-permute-done.17 = bf16[192,2048]{1,0:T(8,128)(2,1)S(1)} collective-permute-done((bf16[192,2048]{1,0:T(8,128)(2,1)S(1)}, bf16[192,2048]{1,0:T(8,128)(2,1)S(1)}, u32[]{:S(2)}, u32[]{:S(2)}) %collective-permute-start.17) | collective-permute-done | bytes 786464 | tf_op jit(solution)/shard_map/ppermute | solution.py:40
  284.8 14.0 %collective-permute-done.2 = bf16[192,2048]{1,0:T(8,128)(2,1)S(1)} collective-permute-done((bf16[192,2048]{1,0:T(8,128)(2,1)S(1)}, bf16[192,2048]{1,0:T(8,128)(2,1)S(1)}, u32[]{:S(2)}, u32[]{:S(2)}) %collective-permute-start.2) | collective-permute-done | bytes 786464 | tf_op jit(solution)/shard_map/ppermute | solution.py:40
  299.3 40.8 %all_to_all.66 = bf16[8,48,2048]{2,1,0:T(8,128)(2,1)S(1)} all-to-all(bf16[8,48,2048]{2,1,0:T(8,128)(2,1)S(1)} %bitcast.249), channel_id=1, replica_groups=mesh['tm'=4,'eg'=2,'sl'=4] {'tm','eg'}, dimensions={0} | all-to-all | bytes 3145728 | tf_op jit(solution)/shard_map/all_to_all | solution.py:44
  341.6 2.5 copy.55
  346.4 19.2 %all_to_all.67 = bf16[32,64,128]{2,1,0:T(8,128)(2,1)S(1)} all-to-all(bf16[32,64,128]{2,1,0:T(8,128)(2,1)S(1)} %bitcast.260), channel_id=1, replica_groups=mesh['tm'=4,'eg'=2,'sl'=4] {'tm','eg','sl'}, dimensions={0} | all-to-all | bytes 1048576 | tf_op jit(solution)/shard_map/all_to_all | solution.py:44
  366.7 2.6 all-to-all-start.6
  369.3 19.8 %weight_grads.1 = (f32[2048,512]{1,0:T(8,128)}, f32[2048,512]{1,0:T(8,128)}, f32[512,2048]{1,0:T(8,128)}) custom-call(bf16[192,2048]{1,0:T(8,128)(2,1)} %bitcast.242, bf16[192,2048]{1,0:T(8,128)(2,1)} %bitcast.247, bf16[192,2048]{1,0:T(8,128)(2,1)} %copy-done.20, bf16[192,2048]{1,0:T(8,128)(2,1)} %copy-done.19, bf16[192,2048]{1,0:T(8,128)(2,1)} %copy-done.21, ...), custom_call_target="tpu_custom_call" | custom-call | tf_op jit(solution)/shard_map/weight_grads/pallas_call | solution.py:74
  389.1 2.1 convolution_convert_fusion.5
  391.2 2.1 copy.62
  393.3 2.3 convolution_convert_fusion.3
  397.0 2.0 copy.63
  399.0 2.0 copy.64
  (216 shorter events, 71.7 us)
Async XLA Ops:
  0.6 174.7 %copy-start = (bf16[1,2048,512]{2,1,0:T(8,128)(2,1)S(1)}, bf16[1,2048,512]{2,1,0:T(8,128)(2,1)}, u32[]{:S(2)}) copy-start(bf16[1,2048,512]{2,1,0:T(8,128)(2,1)} %param.16) | copy-start | bytes 6291460
  3.2 27.2 %copy-start.53 = (f32[128,2]{0,1:T(2,128)S(1)}, f32[128,2]{0,1:T(2,128)}, u32[]{:S(2)}) copy-start(f32[128,2]{0,1:T(2,128)} %param.14) | copy-start | bytes 3076
  3.2 27.5 %copy-start.25 = (bf16[128,2048]{1,0:T(8,128)(2,1)S(1)}, bf16[128,2048]{1,0:T(8,128)(2,1)}, u32[]{:S(2)}) copy-start(bf16[128,2048]{1,0:T(8,128)(2,1)} %param.12) | copy-start | bytes 1572868
  3.2 23.6 %all-to-all-start = ((bf16[32,64,128]{2,1,0:T(8,128)(2,1)}), bf16[32,64,128]{2,1,0:T(8,128)(2,1)S(1)}, u32[]{:S(2)}, u32[]{:S(2)}) async-start(bf16[32,64,128]{2,1,0:T(8,128)(2,1)} %bitcast), calls=%async_computation | async-start | bytes 1048576 | tf_op jit(solution)/shard_map/all_to_all | solution.py:44
  27.8 18.8 %all-to-all-start.1 = ((bf16[32,64,128]{2,1,0:T(8,128)(2,1)}), bf16[32,64,128]{2,1,0:T(8,128)(2,1)S(1)}, u32[]{:S(2)}, u32[]{:S(2)}) async-start(bf16[32,64,128]{2,1,0:T(8,128)(2,1)} %bitcast.2), calls=%async_computation.1 | async-start | bytes 1048576 | tf_op jit(solution)/shard_map/all_to_all | solution.py:44
  46.6 42.7 %all-to-all-start.2 = ((bf16[8,48,2048]{2,1,0:T(8,128)(2,1)}), bf16[8,48,2048]{2,1,0:T(8,128)(2,1)}, u32[]{:S(2)}, u32[]{:S(2)}) async-start(bf16[8,48,2048]{2,1,0:T(8,128)(2,1)} %bitcast.262), calls=%async_computation.2 | async-start | bytes 3145728 | tf_op jit(solution)/shard_map/all_to_all | solution.py:44
  89.3 78.9 %all-to-all-start.3 = ((bf16[8,48,2048]{2,1,0:T(8,128)(2,1)}), bf16[8,48,2048]{2,1,0:T(8,128)(2,1)}, u32[]{:S(2)}, u32[]{:S(2)}) async-start(bf16[8,48,2048]{2,1,0:T(8,128)(2,1)} %bitcast.250), calls=%async_computation.3 | async-start | bytes 3145728 | tf_op jit(solution)/shard_map/all_to_all | solution.py:44
  95.5 37.2 %collective-permute-start.12 = (bf16[192,2048]{1,0:T(8,128)(2,1)S(1)}, bf16[192,2048]{1,0:T(8,128)(2,1)S(1)}, u32[]{:S(2)}, u32[]{:S(2)}) collective-permute-start(bf16[192,2048]{1,0:T(8,128)(2,1)S(1)} %bitcast.234), channel_id=1, source_target_pairs={{0,2},{1,3},{2,0},{3,1},{4,6},{5,7},{6,4},{7,5},{8,10},{9,11},{10,... | collective-permute-start | bytes 2359304 | tf_op jit(solution)/shard_map/ppermute | solution.py:40
  95.6 37.3 %collective-permute-start.3 = (bf16[192,2048]{1,0:T(8,128)(2,1)S(1)}, bf16[192,2048]{1,0:T(8,128)(2,1)S(1)}, u32[]{:S(2)}, u32[]{:S(2)}) collective-permute-start(bf16[192,2048]{1,0:T(8,128)(2,1)S(1)} %bitcast.230), channel_id=1, source_target_pairs={{0,1},{1,0},{2,3},{3,2},{4,5},{5,4},{6,7},{7,6},{8,9},{9,8},{10,11... | collective-permute-start | bytes 2359304 | tf_op jit(solution)/shard_map/ppermute | solution.py:40
  95.8 40.3 %collective-permute-start.9 = (bf16[192,2048]{1,0:T(8,128)(2,1)S(1)}, bf16[192,2048]{1,0:T(8,128)(2,1)S(1)}, u32[]{:S(2)}, u32[]{:S(2)}) collective-permute-start(bf16[192,2048]{1,0:T(8,128)(2,1)S(1)} %bitcast.235), channel_id=1, source_target_pairs={{0,1},{1,0},{2,3},{3,2},{4,5},{5,4},{6,7},{7,6},{8,9},{9,8},{10,11... | collective-permute-start | bytes 2359304 | tf_op jit(solution)/shard_map/ppermute | solution.py:40
  97.7 51.9 %collective-permute-start = (bf16[192,2048]{1,0:T(8,128)(2,1)S(1)}, bf16[192,2048]{1,0:T(8,128)(2,1)S(1)}, u32[]{:S(2)}, u32[]{:S(2)}) collective-permute-start(bf16[192,2048]{1,0:T(8,128)(2,1)S(1)} %bitcast.231), channel_id=1, source_target_pairs={{0,2},{1,3},{2,0},{3,1},{4,6},{5,7},{6,4},{7,5},{8,10},{9,11},{10,... | collective-permute-start | bytes 2359304 | tf_op jit(solution)/shard_map/ppermute | solution.py:40
  132.8 18.5 %collective-permute-start.14 = (bf16[192,2048]{1,0:T(8,128)(2,1)S(1)}, bf16[192,2048]{1,0:T(8,128)(2,1)S(1)}, u32[]{:S(2)}, u32[]{:S(2)}) collective-permute-start(bf16[192,2048]{1,0:T(8,128)(2,1)S(1)} %collective-permute-done.12.refs_13_), channel_id=1, source_target_pairs={{0,1},{1,0},{2,3},{3,2},{4,5},{5,4},{6,7},{7,6},{8,9},{9,8},{10,11... | collective-permute-start | bytes 2359304 | tf_op jit(solution)/shard_map/ppermute | solution.py:40
  132.9 32.8 %collective-permute-start.5 = (bf16[192,2048]{1,0:T(8,128)(2,1)S(1)}, bf16[192,2048]{1,0:T(8,128)(2,1)S(1)}, u32[]{:S(2)}, u32[]{:S(2)}) collective-permute-start(bf16[192,2048]{1,0:T(8,128)(2,1)S(1)} %collective-permute-done.3.refs_10_), channel_id=1, source_target_pairs={{0,2},{1,3},{2,0},{3,1},{4,6},{5,7},{6,4},{7,5},{8,10},{9,11},{10,... | collective-permute-start | bytes 2359304 | tf_op jit(solution)/shard_map/ppermute | solution.py:40
  169.9 24.4 %collective-permute-start.13 = (bf16[192,2048]{1,0:T(8,128)(2,1)S(1)}, bf16[192,2048]{1,0:T(8,128)(2,1)S(1)}, u32[]{:S(2)}, u32[]{:S(2)}) collective-permute-start(bf16[192,2048]{1,0:T(8,128)(2,1)S(1)} %bitcast.243), channel_id=1, source_target_pairs={{0,2},{1,3},{2,0},{3,1},{4,6},{5,7},{6,4},{7,5},{8,10},{9,11},{10,... | collective-permute-start | bytes 2359304 | tf_op jit(solution)/shard_map/ppermute | solution.py:40
  169.9 20.5 %collective-permute-start.10 = (bf16[192,2048]{1,0:T(8,128)(2,1)S(1)}, bf16[192,2048]{1,0:T(8,128)(2,1)S(1)}, u32[]{:S(2)}, u32[]{:S(2)}) collective-permute-start(bf16[192,2048]{1,0:T(8,128)(2,1)S(1)} %bitcast.244), channel_id=1, source_target_pairs={{0,1},{1,0},{2,3},{3,2},{4,5},{5,4},{6,7},{7,6},{8,9},{9,8},{10,11... | collective-permute-start | bytes 2359304 | tf_op jit(solution)/shard_map/ppermute | solution.py:40
  170.9 39.2 %collective-permute-start.4 = (bf16[192,2048]{1,0:T(8,128)(2,1)S(1)}, bf16[192,2048]{1,0:T(8,128)(2,1)S(1)}, u32[]{:S(2)}, u32[]{:S(2)}) collective-permute-start(bf16[192,2048]{1,0:T(8,128)(2,1)S(1)} %bitcast.238), channel_id=1, source_target_pairs={{0,1},{1,0},{2,3},{3,2},{4,5},{5,4},{6,7},{7,6},{8,9},{9,8},{10,11... | collective-permute-start | bytes 2359304 | tf_op jit(solution)/shard_map/ppermute | solution.py:40
  173.3 32.3 %collective-permute-start.1 = (bf16[192,2048]{1,0:T(8,128)(2,1)S(1)}, bf16[192,2048]{1,0:T(8,128)(2,1)S(1)}, u32[]{:S(2)}, u32[]{:S(2)}) collective-permute-start(bf16[192,2048]{1,0:T(8,128)(2,1)S(1)} %bitcast.240), channel_id=1, source_target_pairs={{0,2},{1,3},{2,0},{3,1},{4,6},{5,7},{6,4},{7,5},{8,10},{9,11},{10,... | collective-permute-start | bytes 2359304 | tf_op jit(solution)/shard_map/ppermute | solution.py:40
  178.0 92.1 %copy-start.34 = (bf16[192,512]{1,0:T(8,128)(2,1)}, bf16[192,512]{1,0:T(8,128)(2,1)S(1)}, u32[]{:S(2)}) copy-start(bf16[192,512]{1,0:T(8,128)(2,1)S(1)} %get-tuple-element.59.refs_32_) | copy-start | bytes 589828
  194.1 76.9 %collective-permute-start.11 = (bf16[192,2048]{1,0:T(8,128)(2,1)S(1)}, bf16[192,2048]{1,0:T(8,128)(2,1)S(1)}, u32[]{:S(2)}, u32[]{:S(2)}) collective-permute-start(bf16[192,2048]{1,0:T(8,128)(2,1)S(1)} %fusion.2), channel_id=1, source_target_pairs={{0,1},{1,0},{2,3},{3,2},{4,5},{5,4},{6,7},{7,6},{8,9},{9,8},{10,11... | collective-permute-start | bytes 2359304 | tf_op jit(solution)/shard_map/ppermute | solution.py:40
  194.3 45.1 %collective-permute-start.15 = (bf16[192,2048]{1,0:T(8,128)(2,1)S(1)}, bf16[192,2048]{1,0:T(8,128)(2,1)S(1)}, u32[]{:S(2)}, u32[]{:S(2)}) collective-permute-start(bf16[192,2048]{1,0:T(8,128)(2,1)S(1)} %collective-permute-done.13.refs_5_), channel_id=1, source_target_pairs={{0,1},{1,0},{2,3},{3,2},{4,5},{5,4},{6,7},{7,6},{8,9},{9,8},{10,11... | collective-permute-start | bytes 2359304 | tf_op jit(solution)/shard_map/ppermute | solution.py:40
  210.0 33.3 %collective-permute-start.6 = (bf16[192,2048]{1,0:T(8,128)(2,1)S(1)}, bf16[192,2048]{1,0:T(8,128)(2,1)S(1)}, u32[]{:S(2)}, u32[]{:S(2)}) collective-permute-start(bf16[192,2048]{1,0:T(8,128)(2,1)S(1)} %collective-permute-done.4.refs_2_), channel_id=1, source_target_pairs={{0,2},{1,3},{2,0},{3,1},{4,6},{5,7},{6,4},{7,5},{8,10},{9,11},{10,... | collective-permute-start | bytes 2359304 | tf_op jit(solution)/shard_map/ppermute | solution.py:40
  212.6 36.2 %copy-start.37 = (bf16[192,512]{1,0:T(8,128)(2,1)}, bf16[192,512]{1,0:T(8,128)(2,1)S(1)}, u32[]{:S(2)}) copy-start(bf16[192,512]{1,0:T(8,128)(2,1)S(1)} %get-tuple-element.43.refs_29_) | copy-start | bytes 589828
  212.6 48.5 %copy-start.38 = (bf16[192,512]{1,0:T(8,128)(2,1)}, bf16[192,512]{1,0:T(8,128)(2,1)S(1)}, u32[]{:S(2)}) copy-start(bf16[192,512]{1,0:T(8,128)(2,1)S(1)} %get-tuple-element.44.refs_37_) | copy-start | bytes 589828
  214.0 49.4 %copy-start.39 = (bf16[192,512]{1,0:T(8,128)(2,1)}, bf16[192,512]{1,0:T(8,128)(2,1)S(1)}, u32[]{:S(2)}) copy-start(bf16[192,512]{1,0:T(8,128)(2,1)S(1)} %get-tuple-element.52.refs_26_) | copy-start | bytes 589828
  214.0 53.6 %copy-start.40 = (bf16[192,512]{1,0:T(8,128)(2,1)}, bf16[192,512]{1,0:T(8,128)(2,1)S(1)}, u32[]{:S(2)}) copy-start(bf16[192,512]{1,0:T(8,128)(2,1)S(1)} %get-tuple-element.53.refs_34_) | copy-start | bytes 589828
  243.0 18.0 %collective-permute-start.16 = (bf16[192,2048]{1,0:T(8,128)(2,1)S(1)}, bf16[192,2048]{1,0:T(8,128)(2,1)S(1)}, u32[]{:S(2)}, u32[]{:S(2)}) collective-permute-start(bf16[192,2048]{1,0:T(8,128)(2,1)S(1)} %fusion.3), channel_id=1, source_target_pairs={{0,1},{1,0},{2,3},{3,2},{4,5},{5,4},{6,7},{7,6},{8,9},{9,8},{10,11... | collective-permute-start | bytes 2359304 | tf_op jit(solution)/shard_map/ppermute | solution.py:40
  247.1 20.5 %collective-permute-start.7 = (bf16[192,2048]{1,0:T(8,128)(2,1)S(1)}, bf16[192,2048]{1,0:T(8,128)(2,1)S(1)}, u32[]{:S(2)}, u32[]{:S(2)}) collective-permute-start(bf16[192,2048]{1,0:T(8,128)(2,1)S(1)} %fusion.1), channel_id=1, source_target_pairs={{0,2},{1,3},{2,0},{3,1},{4,6},{5,7},{6,4},{7,5},{8,10},{9,11},{10,... | collective-permute-start | bytes 2359304 | tf_op jit(solution)/shard_map/ppermute | solution.py:40
  261.9 22.5 %collective-permute-start.17 = (bf16[192,2048]{1,0:T(8,128)(2,1)S(1)}, bf16[192,2048]{1,0:T(8,128)(2,1)S(1)}, u32[]{:S(2)}, u32[]{:S(2)}) collective-permute-start(bf16[192,2048]{1,0:T(8,128)(2,1)S(1)} %add_convert_fusion.1), channel_id=1, source_target_pairs={{0,2},{1,3},{2,0},{3,1},{4,6},{5,7},{6,4},{7,5},{8,10},{9,11},{10,... | collective-permute-start | bytes 2359304 | tf_op jit(solution)/shard_map/ppermute | solution.py:40
  264.2 34.6 %collective-permute-start.2 = (bf16[192,2048]{1,0:T(8,128)(2,1)S(1)}, bf16[192,2048]{1,0:T(8,128)(2,1)S(1)}, u32[]{:S(2)}, u32[]{:S(2)}) collective-permute-start(bf16[192,2048]{1,0:T(8,128)(2,1)S(1)} %fusion), channel_id=1, source_target_pairs={{0,2},{1,3},{2,0},{3,1},{4,6},{5,7},{6,4},{7,5},{8,10},{9,11},{10,... | collective-permute-start | bytes 2359304 | tf_op jit(solution)/shard_map/ppermute | solution.py:40
  268.4 30.4 %collective-permute-start.8 = (bf16[192,2048]{1,0:T(8,128)(2,1)S(1)}, bf16[192,2048]{1,0:T(8,128)(2,1)S(1)}, u32[]{:S(2)}, u32[]{:S(2)}) collective-permute-start(bf16[192,2048]{1,0:T(8,128)(2,1)S(1)} %add_convert_fusion.3), channel_id=1, source_target_pairs={{0,1},{1,0},{2,3},{3,2},{4,5},{5,4},{6,7},{7,6},{8,9},{9,8},{10,11... | collective-permute-start | bytes 2359304 | tf_op jit(solution)/shard_map/ppermute | solution.py:40
  299.3 40.8 %copy-start.26 = (bf16[128,2048]{1,0:T(8,128)(2,1)S(1)}, bf16[128,2048]{1,0:T(8,128)(2,1)}, u32[]{:S(2)}) copy-start(bf16[128,2048]{1,0:T(8,128)(2,1)} %param.12) | copy-start | bytes 1572868
  366.7 26.6 %all-to-all-start.6 = ((bf16[32,64,128]{2,1,0:T(8,128)(2,1)}), bf16[32,64,128]{2,1,0:T(8,128)(2,1)S(1)}, u32[]{:S(2)}, u32[]{:S(2)}) async-start(bf16[32,64,128]{2,1,0:T(8,128)(2,1)} %bitcast.27), calls=%async_computation.6 | async-start | bytes 1048576 | tf_op jit(solution)/shard_map/all_to_all | solution.py:44
  (45 other events, 263.2 us)
